TPU v7x, 512 devices: a whole 4x4x16 slice. The times are simulated.
512 devices in a mesh: section: 4 (over x), doc: 32 (over z, core), mp: 4 (over y).
Axes of the slice: x: 4, y: 4, z: 16, core: 2. Of those that a mesh axis runs over, the one named last changes fastest.
Arguments:
- queries: bfloat16 [64, 512, 8, 4, 128], P('doc', None, 'section', 'mp'), may hold values from -420 to 420
- cotangent: bfloat16 [64, 512, 8, 4, 128], P('doc', None, 'section', 'mp'), may hold values from -180 to 180
- cache: bfloat16 [512, 128, 4, 2, 128], P('doc', 'section', 'mp'), may hold values from -7 to 7
- momentum: float32 [512, 128, 4, 2, 128], P('doc', 'section', 'mp'), may hold values from -3 to 3
- doc_lists: int32 [64, 8], P('doc'), may hold values from 0 to 511, as said below
- place: int32 [512], replicated, may hold values from 0 to 511, as said below
Outputs:
- attention: bfloat16 [64, 512, 8, 4, 128], P('doc', None, 'section', 'mp')
- new_cache: bfloat16 [512, 128, 4, 2, 128], P('doc', 'section', 'mp')
- new_momentum: float32 [512, 128, 4, 2, 128], P('doc', 'section', 'mp')
Inputs may be any that keep to these rules, and one draw needn't show every extreme that they name: `doc_lists`: the 2 rows of one index of doc (an aligned block of rows) name 16 different documents in all. Counting each document's owner as place[document] // 16, those documents lie on at most 1 per owner. `place`: each row of cache holds exactly one document.
All inputs are finite; a program needn't handle non-finite values.
Results may differ from a plain program's by a relative error of at most 0.017.
Values may be sent and summed in bfloat16 or wider, within the bound.
No kernel may reach another device: no remote copies, remote signals or barrier semaphores. Data moves between devices by JAX's collectives and lax.ppermute only.
A program may use at most 64 MiB of HBM per device.

v0:
```python
import math
import jax
import jax.numpy as jnp
from jax import lax
from jax.sharding import PartitionSpec as P

momentum_decay = 0.9
step_rate = 0.3
clip_level = 0.5


def body(queries, cotangent, cache, momentum, doc_lists, place):
    rows_dev, seq_len, head_count, kv_count, head_size = queries.shape
    doc_dev, len_part = (cache.shape[0], cache.shape[1])
    doc_total = place.shape[0]
    owners = doc_total // doc_dev
    sections = lax.axis_size("section")
    list_len = doc_lists.shape[1]
    requests = rows_dev * list_len
    owner_used = min(owners, requests)
    capacity = (requests + owner_used - 1) // owner_used
    flat_width = kv_count * 2 * head_size
    score_scale = 1.0 / math.sqrt(head_size)
    everyone = lax.all_gather(doc_lists, "doc", axis=0, tiled=True).reshape(owners, requests)
    matches = (
        everyone[:, :, None] == jnp.arange(doc_total, dtype=jnp.int32)[None, None, :]
    ).astype(jnp.int32)
    positions = jnp.sum(matches * place[None, None, :], axis=-1)
    holder = positions // doc_dev
    local_slot = positions % doc_dev
    earlier = jnp.arange(requests)[:, None] > jnp.arange(requests)[None, :]
    same_owner = holder[:, :, None] == holder[:, None, :]
    slot_rank = jnp.sum((same_owner & earlier[None]).astype(jnp.int32), axis=-1)
    my_index = lax.axis_index("doc")
    my_holder = lax.dynamic_index_in_dim(holder, my_index, 0, keepdims=False)
    my_rank = lax.dynamic_index_in_dim(slot_rank, my_index, 0, keepdims=False)
    target = my_holder * capacity + my_rank
    claimed = (holder == my_index)[:, :, None] & (
        slot_rank[:, :, None] == jnp.arange(capacity)[None, None, :]
    )
    slot_table = jnp.sum(jnp.where(claimed, local_slot[:, :, None], 0), axis=1)
    filled = jnp.any(claimed, axis=1)
    stored = cache.reshape(doc_dev, len_part, flat_width)
    outgoing = jnp.where(filled[:, :, None, None], stored[slot_table], jnp.zeros((), jnp.bfloat16))
    fanned = jnp.broadcast_to(outgoing[None], (sections,) + outgoing.shape)
    fanned = fanned.reshape(sections * owners, capacity, len_part, flat_width)
    arrived = lax.all_to_all(fanned, ("section", "doc"), split_axis=0, concat_axis=0, tiled=True)
    arrived = arrived.reshape(sections, owners * capacity, len_part, flat_width)
    picked = arrived[:, target]
    fetched = jnp.moveaxis(picked, 0, 1).reshape(requests, sections * len_part, flat_width)
    length = fetched.shape[1]
    memory = fetched.reshape(rows_dev, list_len * length, kv_count, 2, head_size)

    def row_attention(operands):
        query_row, tangent_row, memory_row = operands
        query = query_row[:, :, 0, :].reshape(seq_len * head_count, head_size)
        tangent = tangent_row[:, :, 0, :].reshape(seq_len * head_count, head_size)
        key_rows = memory_row[:, 0, 0, :]
        value_rows = memory_row[:, 0, 1, :]
        scores = (
            jnp.einsum("qd,kd->qk", query, key_rows, preferred_element_type=jnp.float32)
            * score_scale
        )
        weights = jax.nn.softmax(scores, axis=-1)
        weight_bf = weights.astype(jnp.bfloat16)
        attended = jnp.dot(weight_bf, value_rows, preferred_element_type=jnp.float32).astype(
            jnp.bfloat16
        )
        row_delta = jnp.sum(
            attended.astype(jnp.float32) * tangent.astype(jnp.float32), axis=-1, keepdims=True
        )
        grad_weights = jnp.einsum(
            "qd,kd->qk", tangent, value_rows, preferred_element_type=jnp.float32
        )
        grad_scores = (weights * (grad_weights - row_delta) * score_scale).astype(jnp.bfloat16)
        grad_keys = jnp.einsum("qk,qd->kd", grad_scores, query, preferred_element_type=jnp.float32)
        grad_values = jnp.einsum(
            "qk,qd->kd", weight_bf, tangent, preferred_element_type=jnp.float32
        )
        grad_list = [jnp.stack([grad_keys, grad_values], axis=1).astype(jnp.bfloat16)]
        attended_list = [attended.reshape(seq_len, head_count, head_size)]
        return (jnp.stack(attended_list, axis=2), jnp.stack(grad_list, axis=1))

    attention, partial_value = lax.map(row_attention, (queries, cotangent, memory))
    partial_value = partial_value.reshape(requests, length, flat_width)
    pieces = partial_value.reshape(requests, sections, len_part, flat_width)
    parcel = (
        jnp.zeros((owners * capacity, sections, len_part, flat_width), jnp.bfloat16)
        .at[target]
        .set(pieces)
    )
    parcel = jnp.moveaxis(parcel, 1, 0).reshape(sections * owners, capacity, len_part, flat_width)
    returned = lax.all_to_all(parcel, ("section", "doc"), split_axis=0, concat_axis=0, tiled=True)
    returned = returned.reshape(sections, owners * capacity, len_part * flat_width).astype(
        jnp.float32
    )
    collected = jnp.sum(returned, axis=0)
    assign = (slot_table.reshape(-1)[None, :] == jnp.arange(doc_dev)[:, None]) & filled.reshape(-1)[
        None, :
    ]
    gradient = jnp.dot(
        assign.astype(jnp.float32),
        collected,
        precision=lax.Precision.HIGHEST,
        preferred_element_type=jnp.float32,
    )
    gradient = gradient.reshape(momentum.shape)
    norm_square = lax.psum(jnp.sum(gradient * gradient), ("section", "doc", "mp"))
    entry_count = doc_total * len_part * sections * kv_count * lax.axis_size("mp") * 2 * head_size
    clip_limit = clip_level * math.sqrt(entry_count)
    norm_value = jnp.sqrt(norm_square)
    factor = clip_limit / jnp.maximum(norm_value, clip_limit)
    new_momentum = momentum_decay * momentum + factor * gradient
    new_cache = (cache.astype(jnp.float32) - step_rate * new_momentum).astype(jnp.bfloat16)
    return (attention, new_cache, new_momentum)


def solution(mesh):
    in_specs = (
        P("doc", None, "section", "mp", None),
        P("doc", None, "section", "mp", None),
        P("doc", "section", "mp", None, None),
        P("doc", "section", "mp", None, None),
        P("doc", None),
        P(),
    )
    out_specs = (
        P("doc", None, "section", "mp", None),
        P("doc", "section", "mp", None, None),
        P("doc", "section", "mp", None, None),
    )
    return jax.shard_map(body, mesh=mesh, in_specs=in_specs, out_specs=out_specs, check_vma=False)
```

profile of v0, /device:TPU:1, one launch (start us, length us, event | category | flops | bytes accessed | tf_op | source)
XLA Modules:
  0.0 404.3 jit_solution(12242166268992438319)
XLA Ops:
  0.6 37.9 %all-gather = s32[32,2,8]{2,1,0:T(2,128)S(1)} all-gather(s32[1,2,8]{2,1,0:T(2,128)} %bitcast.94), channel_id=1, replica_groups=mesh['section'=4,'doc'=32,'mp'=4] {'doc'}, dimensions={0}, use_global_device_ids=true | all-gather | bytes 2112 | tf_op jit(solution)/shard_map/all_gather | solution.py:24
  38.7 1.4 select_reduce_fusion
  40.7 1.1 reshape.202
  42.5 1.6 broadcast_in_dim.32
  44.1 10.6 %all-to-all-start = ((bf16[128,1,32,256]{3,2,1,0:T(8,128)(2,1)}), bf16[128,1,32,256]{3,2,1,0:T(8,128)(2,1)S(1)}, u32[]{:S(2)}, u32[]{:S(2)}) async-start(bf16[128,1,32,256]{3,2,1,0:T(8,128)(2,1)} %bitcast.12), calls=%async_computation | async-start | bytes 4194304 | tf_op jit(solution)/shard_map/all_to_all | solution.py:47
  54.8 99.1 %all-to-all-done = bf16[128,1,32,256]{3,2,1,0:T(8,128)(2,1)S(1)} async-done(((bf16[128,1,32,256]{3,2,1,0:T(8,128)(2,1)}), bf16[128,1,32,256]{3,2,1,0:T(8,128)(2,1)S(1)}, u32[]{:S(2)}, u32[]{:S(2)}) %all-to-all-start) | async-done | bytes 2097184 | tf_op jit(solution)/shard_map/all_to_all | solution.py:47
  154.8 28.1 %while.12 = (s32[]{:T(128)}, bf16[2,512,2,1,128]{4,2,1,3,0:T(2,128)(2,1)}, bf16[2,1024,1,2,128]{4,3,1,0,2:T(2,128)(2,1)}, bf16[2,512,2,1,128]{4,2,3,1,0:T(2,128)...) while((s32[]{:T(128)}, ...), condition=%wide.region_8.9_spmd, body=%wide.region_4.8_spmd.sunk | while | flops 1364325376 | bytes 61124872 | solution.py:84
  155.3 1.1 constant_dynamic-slice_fusion.8
  158.1 1.3 multiply_reduce_fusion.6
  159.4 3.6 fusion.45
  163.0 3.2 fusion.44
  166.9 1.0 copy-done.3
  169.4 1.1 constant_dynamic-slice_fusion.8
  172.2 1.3 multiply_reduce_fusion.6
  173.4 3.6 fusion.45
  177.1 3.2 fusion.44
  183.0 1.7 reshape.226
  185.0 1.1 scatter_fusion
  186.3 107.8 %all_to_all.10 = bf16[128,1,32,256]{3,2,1,0:T(8,128)(2,1)S(1)} all-to-all(bf16[128,1,32,256]{3,2,1,0:T(8,128)(2,1)S(1)} %bitcast.86), channel_id=1, replica_groups=mesh['section'=4,'doc'=32,'mp'=4] {'section','doc'}, dimensions={0} | all-to-all | bytes 4194304 | tf_op jit(solution)/shard_map/all_to_all | solution.py:93
  294.1 2.8 reshape.205
  296.8 2.6 reduce_sum.69
  299.4 1.2 multiply_reduce_fusion.2
  300.6 100.9 %psum.7 = f32[]{:T(128)} all-reduce(f32[]{:T(128)} %get-tuple-element.103), channel_id=1, replica_groups=mesh['section'=4,'doc'=32,'mp'=4] {'section','doc','mp'}, use_global_device_ids=true, to_apply=%region_12.13 | all-reduce | flops 1 | bytes 8 | tf_op jit(solution)/shard_map/psum | solution.py:108
  402.8 1.5 subtract_convert_fusion
  (66 shorter events, 11.6 us)
Async XLA Ops:
  44.1 109.8 %all-to-all-start = ((bf16[128,1,32,256]{3,2,1,0:T(8,128)(2,1)}), bf16[128,1,32,256]{3,2,1,0:T(8,128)(2,1)S(1)}, u32[]{:S(2)}, u32[]{:S(2)}) async-start(bf16[128,1,32,256]{3,2,1,0:T(8,128)(2,1)} %bitcast.12), calls=%async_computation | async-start | bytes 4194304 | tf_op jit(solution)/shard_map/all_to_all | solution.py:47
  156.4 1.5 copy-start.1
  157.1 2.3 copy-start
  163.0 3.3 copy-start.2
  163.0 4.9 %copy-start.6 = (bf16[2,512,2,1,128]{4,2,1,3,0:T(2,128)(2,1)S(1)}, bf16[2,512,2,1,128]{4,2,1,3,0:T(2,128)(2,1)}, u32[]{:S(2)}) copy-start(bf16[2,512,2,1,128]{4,2,1,3,0:T(2,128)(2,1)} %get-tuple-element.158) | copy-start | bytes 1572868 | tf_op jit(solution)/shard_map/while
  166.9 1.0 copy-start.3
  168.1 0.8 copy-start.7
  170.5 1.5 copy-start.1
  171.2 2.2 copy-start
  177.1 3.3 copy-start.2
  177.1 4.9 %copy-start.6 = (bf16[2,512,2,1,128]{4,2,1,3,0:T(2,128)(2,1)S(1)}, bf16[2,512,2,1,128]{4,2,1,3,0:T(2,128)(2,1)}, u32[]{:S(2)}) copy-start(bf16[2,512,2,1,128]{4,2,1,3,0:T(2,128)(2,1)} %get-tuple-element.158) | copy-start | bytes 1572868 | tf_op jit(solution)/shard_map/while
  181.0 1.0 copy-start.3
  182.2 0.8 copy-start.7
  296.8 105.9 %copy-start.4 = (bf16[16,32,1,2,128]{4,3,2,1,0:T(2,128)(2,1)S(1)}, bf16[16,32,1,2,128]{4,3,2,1,0:T(2,128)(2,1)}, u32[]{:S(2)}) copy-start(bf16[16,32,1,2,128]{4,3,2,1,0:T(2,128)(2,1)} %param.10) | copy-start | bytes 786436
  296.8 105.9 %copy-start.5 = (f32[16,32,1,2,128]{4,3,2,1,0:T(2,128)S(1)}, f32[16,32,1,2,128]{4,3,2,1,0:T(2,128)}, u32[]{:S(2)}) copy-start(f32[16,32,1,2,128]{4,3,2,1,0:T(2,128)} %param.11) | copy-start | bytes 1572868
where the time goes:
time: 405 us; the launch traced here: 404 us
  blocking collectives  247 us (61%)
  waiting for transfers between devices  99.1 us (24%)
  local copies, waits for them, and re-layouts  19.7 us (5%)
  matrix products  18.8 us (5%)
  starting transfers between devices  10.6 us (3%)
  other arithmetic  7.65 us (2%)
    all_to_all x1, blocking collectives, body(): lax.all_to_all(parcel, ('section', 'doc'), split_axis=0, concat_axis=0, t...  108 us
    psum x1, blocking collectives, body(): lax.psum(jnp.sum(gradient * gradient), ('section', 'doc', 'mp'))  101 us
    all_to_all x1, waiting for transfers between devices, body(): lax.all_to_all(fanned, ('section', 'doc'), split_axis=0, concat_axis=0, t...  99.1 us
    all_gather x1, blocking collectives, body(): lax.all_gather(doc_lists, 'doc', axis=0, tiled=True)  37.9 us
    all_to_all x1, starting transfers between devices, body(): lax.all_to_all(fanned, ('section', 'doc'), split_axis=0, concat_axis=0, t...  10.6 us
  transfers between devices with their start and end apart: 1, of which 1 were waited for; matrix products, arithmetic and copies ran while one was open for 0% of the time, Pallas kernels for 0%

commit v1 on v0

--- a/solution.py
+++ b/solution.py
@@ -21,7 +21,9 @@
     capacity = (requests + owner_used - 1) // owner_used
     flat_width = kv_count * 2 * head_size
     score_scale = 1.0 / math.sqrt(head_size)
-    everyone = lax.all_gather(doc_lists, "doc", axis=0, tiled=True).reshape(owners, requests)
+    everyone = jnp.concatenate(
+        lax.all_to_all(jnp.stack([doc_lists] * lax.axis_size("doc")), "doc", 0, 0), axis=0
+    ).reshape(owners, requests)
     matches = (
         everyone[:, :, None] == jnp.arange(doc_total, dtype=jnp.int32)[None, None, :]
     ).astype(jnp.int32)

time: 405 us -> 392 us (0.968)
  blocking collectives: 247 us -> 209 us
  starting transfers between devices: 10.6 us -> 23.5 us
  waiting for transfers between devices: 99.1 us -> 110 us
    all_gather x1 -> x0, blocking collectives: 37.9 us -> none  [body(): lax.all_gather(doc_lists, 'doc', axis=0, tiled=True)]
    all_to_all x0 -> x1, starting transfers between devices: none -> 16.7 us  [body(): lax.all_to_all(jnp.stack([doc_lists] * lax.axis_size('doc')), 'doc', 0, 0)]
    all_to_all x0 -> x1, waiting for transfers between devices: none -> 10.9 us  [body(): lax.all_to_all(jnp.stack([doc_lists] * lax.axis_size('doc')), 'doc', 0, 0)]
  transfers between devices with their start and end apart: 1 -> 2, of which waited for: 1 -> 2; matrix products, arithmetic and copies ran while one was open for 0% -> 0% of each run, Pallas kernels for 0% -> 0%
where the time goes in v1:
time: 392 us
  blocking collectives  209 us (53%)
  waiting for transfers between devices  110 us (28%)
  starting transfers between devices  23.5 us (6%)
  local copies, waits for them, and re-layouts  21 us (5%)
  matrix products  18.8 us (5%)
  other arithmetic  7.65 us (2%)
    all_to_all x1, blocking collectives, body(): lax.all_to_all(parcel, ('section', 'doc'), split_axis=0, concat_axis=0, t...  108 us
    psum x1, blocking collectives, body(): lax.psum(jnp.sum(gradient * gradient), ('section', 'doc', 'mp'))  101 us
    all_to_all x1, waiting for transfers between devices, body(): lax.all_to_all(fanned, ('section', 'doc'), split_axis=0, concat_axis=0, t...  99.1 us
    all_to_all x1, starting transfers between devices, body(): lax.all_to_all(jnp.stack([doc_lists] * lax.axis_size('doc')), 'doc', 0, 0)  16.7 us
    all_to_all x1, waiting for transfers between devices, body(): lax.all_to_all(jnp.stack([doc_lists] * lax.axis_size('doc')), 'doc', 0, 0)  10.9 us
  transfers between devices with their start and end apart: 2, of which 2 were waited for; matrix products, arithmetic and copies ran while one was open for 0% of the time, Pallas kernels for 0%

profile of v1, /device:TPU:1, one launch (start us, length us, event | category | flops | bytes accessed | tf_op | source)
XLA Modules:
  0.0 391.6 jit_solution(4313722544463272879)
XLA Ops:
  0.6 1.3 stack.8
  1.9 16.7 %all-to-all-start = ((s32[32,2,8]{2,1,0:T(2,128)}), s32[32,2,8]{2,1,0:T(2,128)S(1)}, u32[]{:S(2)}, u32[]{:S(2)}) async-start(s32[32,2,8]{2,1,0:T(2,128)} %stack.8), calls=%async_computation | async-start | bytes 65536 | tf_op jit(solution)/shard_map/all_to_all | solution.py:25
  19.8 10.9 %all-to-all-done = s32[32,2,8]{2,1,0:T(2,128)S(1)} async-done(((s32[32,2,8]{2,1,0:T(2,128)}), s32[32,2,8]{2,1,0:T(2,128)S(1)}, u32[]{:S(2)}, u32[]{:S(2)}) %all-to-all-start) | async-done | bytes 2080 | tf_op jit(solution)/shard_map/all_to_all | solution.py:25
  30.9 1.4 select_reduce_fusion
  33.5 1.6 broadcast_in_dim.32
  35.2 6.8 %all-to-all-start.1 = ((bf16[128,1,32,256]{3,2,1,0:T(8,128)(2,1)}), bf16[128,1,32,256]{3,2,1,0:T(8,128)(2,1)S(1)}, u32[]{:S(2)}, u32[]{:S(2)}) async-start(bf16[128,1,32,256]{3,2,1,0:T(8,128)(2,1)} %bitcast.11), calls=%async_computation.1 | async-start | bytes 4194304 | tf_op jit(solution)/shard_map/all_to_all | solution.py:49
  42.0 99.1 %all-to-all-done.1 = bf16[128,1,32,256]{3,2,1,0:T(8,128)(2,1)S(1)} async-done(((bf16[128,1,32,256]{3,2,1,0:T(8,128)(2,1)}), bf16[128,1,32,256]{3,2,1,0:T(8,128)(2,1)S(1)}, u32[]{:S(2)}, u32[]{:S(2)}) %all-to-all-start.1) | async-done | bytes 2097184 | tf_op jit(solution)/shard_map/all_to_all | solution.py:49
  142.1 28.1 %while.12 = (s32[]{:T(128)}, bf16[2,512,2,1,128]{4,2,1,3,0:T(2,128)(2,1)}, bf16[2,1024,1,2,128]{4,3,1,0,2:T(2,128)(2,1)}, bf16[2,512,2,1,128]{4,2,3,1,0:T(2,128)...) while((s32[]{:T(128)}, ...), condition=%wide.region_8.9_spmd, body=%wide.region_4.8_spmd.sunk | while | flops 1364325376 | bytes 61124872 | solution.py:86
  142.5 1.1 constant_dynamic-slice_fusion.8
  145.4 1.3 multiply_reduce_fusion.6
  146.6 3.6 fusion.45
  150.3 3.2 fusion.44
  156.6 1.1 constant_dynamic-slice_fusion.8
  159.4 1.3 multiply_reduce_fusion.6
  160.7 3.6 fusion.45
  164.3 3.2 fusion.44
  170.2 1.7 reshape.228
  172.2 1.1 scatter_fusion
  173.5 107.8 %all_to_all.15 = bf16[128,1,32,256]{3,2,1,0:T(8,128)(2,1)S(1)} all-to-all(bf16[128,1,32,256]{3,2,1,0:T(8,128)(2,1)S(1)} %bitcast.85), channel_id=1, replica_groups=mesh['section'=4,'doc'=32,'mp'=4] {'section','doc'}, dimensions={0} | all-to-all | bytes 4194304 | tf_op jit(solution)/shard_map/all_to_all | solution.py:95
  281.3 2.8 reshape.207
  284.1 2.6 reduce_sum.69
  286.6 1.2 multiply_reduce_fusion.2
  287.8 101.0 %psum.7 = f32[]{:T(128)} all-reduce(f32[]{:T(128)} %get-tuple-element.103), channel_id=1, replica_groups=mesh['section'=4,'doc'=32,'mp'=4] {'section','doc','mp'}, use_global_device_ids=true, to_apply=%region_12.13 | all-reduce | flops 1 | bytes 8 | tf_op jit(solution)/shard_map/psum | solution.py:110
  390.0 1.5 subtract_convert_fusion
  (68 shorter events, 13.7 us)
Async XLA Ops:
  1.9 28.8 %all-to-all-start = ((s32[32,2,8]{2,1,0:T(2,128)}), s32[32,2,8]{2,1,0:T(2,128)S(1)}, u32[]{:S(2)}, u32[]{:S(2)}) async-start(s32[32,2,8]{2,1,0:T(2,128)} %stack.8), calls=%async_computation | async-start | bytes 65536 | tf_op jit(solution)/shard_map/all_to_all | solution.py:25
  35.2 106.0 %all-to-all-start.1 = ((bf16[128,1,32,256]{3,2,1,0:T(8,128)(2,1)}), bf16[128,1,32,256]{3,2,1,0:T(8,128)(2,1)S(1)}, u32[]{:S(2)}, u32[]{:S(2)}) async-start(bf16[128,1,32,256]{3,2,1,0:T(8,128)(2,1)} %bitcast.11), calls=%async_computation.1 | async-start | bytes 4194304 | tf_op jit(solution)/shard_map/all_to_all | solution.py:49
  143.7 1.5 copy-start.1
  144.4 2.2 copy-start
  150.2 3.3 copy-start.2
  150.2 4.9 %copy-start.6 = (bf16[2,512,2,1,128]{4,2,1,3,0:T(2,128)(2,1)S(1)}, bf16[2,512,2,1,128]{4,2,1,3,0:T(2,128)(2,1)}, u32[]{:S(2)}) copy-start(bf16[2,512,2,1,128]{4,2,1,3,0:T(2,128)(2,1)} %get-tuple-element.158) | copy-start | bytes 1572868 | tf_op jit(solution)/shard_map/while
  154.1 1.0 copy-start.3
  155.3 0.8 copy-start.7
  157.7 1.5 copy-start.1
  158.4 2.3 copy-start
  164.3 3.3 copy-start.2
  164.3 4.9 %copy-start.6 = (bf16[2,512,2,1,128]{4,2,1,3,0:T(2,128)(2,1)S(1)}, bf16[2,512,2,1,128]{4,2,1,3,0:T(2,128)(2,1)}, u32[]{:S(2)}) copy-start(bf16[2,512,2,1,128]{4,2,1,3,0:T(2,128)(2,1)} %get-tuple-element.158) | copy-start | bytes 1572868 | tf_op jit(solution)/shard_map/while
  168.2 1.0 copy-start.3
  169.4 0.8 copy-start.7
  284.0 106.0 %copy-start.4 = (bf16[16,32,1,2,128]{4,3,2,1,0:T(2,128)(2,1)S(1)}, bf16[16,32,1,2,128]{4,3,2,1,0:T(2,128)(2,1)}, u32[]{:S(2)}) copy-start(bf16[16,32,1,2,128]{4,3,2,1,0:T(2,128)(2,1)} %param.10) | copy-start | bytes 786436
  284.1 106.0 %copy-start.5 = (f32[16,32,1,2,128]{4,3,2,1,0:T(2,128)S(1)}, f32[16,32,1,2,128]{4,3,2,1,0:T(2,128)}, u32[]{:S(2)}) copy-start(f32[16,32,1,2,128]{4,3,2,1,0:T(2,128)} %param.11) | copy-start | bytes 1572868
